TPU v7x, 256 devices: a whole 4x4x8 slice. The times are simulated.
256 devices in a mesh: band: 4 (over x), dom: 64 (over z, y, core).
Axes of the slice: x: 4, y: 4, z: 8, core: 2. Of those that a mesh axis runs over, the one named last changes fastest.
Arguments:
- orbitals: bfloat16 [256, 512, 2048], P('dom', None, 'band'), may hold values from -6 to 6
- projector_blocks: bfloat16 [4, 64, 96, 256, 128], P('band', 'dom'), may hold values from -0.1875 to 0.1875
- block_rows: int32 [4, 64, 96], P('band', 'dom'), may hold values from 0 to 15, as said below
- block_cols: int32 [4, 64, 96], P('band', 'dom'), may hold values from 0 to 26
- block_counts: int32 [4, 64], P('band', 'dom'), may hold values from 16 to 96, as said below
- strengths: float32 [73728], P('dom'), may hold values from -1.5 to 1.5
Outputs:
- applied: bfloat16 [256, 512, 2048], P('dom', None, 'band')
Inputs may be any that keep to these rules, and one draw needn't show every extreme that they name: `block_rows`: the slots of one device name distinct pairs of row block and column block. `block_counts`: some device has all 96 slots live.
All inputs are finite; a program needn't handle non-finite values.
Results may differ from a plain program's by a relative error of at most 0.0049.
Values may be sent and summed in bfloat16 or wider, within the bound.
A program may use at most 128 MiB of HBM per device.

v0:
```python
import jax
import jax.numpy as jnp
from jax import lax
from jax.sharding import PartitionSpec as P


def passed_along(value, axis, steps):
    count = lax.axis_size(axis)
    pairs = [(source, (source + steps) % count) for source in range(count)]
    return lax.ppermute(value, axis, pairs)


def padded(shard, sides, width):
    for axis, dim in sides:
        size, length = (lax.axis_size(axis), shard.shape[dim])
        up = [(i, (i + 1) % size) for i in range(size)]
        down = [(j, i) for i, j in up]
        last = lax.slice_in_dim(shard, length - width, length, axis=dim)
        leading = lax.slice_in_dim(shard, 0, width, axis=dim)
        before = lax.ppermute(last, axis, up)
        after = lax.ppermute(leading, axis, down)
        shard = jnp.concatenate([before, shard, after], axis=dim)
    return shard


def per_device(orbitals, projector_blocks, block_rows, block_cols, block_counts, strengths):
    slab_states = lax.all_to_all(orbitals, "dom", split_axis=1, concat_axis=0, tiled=True)
    state_total = slab_states.shape[0]
    planes = slab_states.shape[1]
    points = slab_states.shape[2]
    weights = projector_blocks[0, 0]
    slot_total = weights.shape[0]
    row_width = weights.shape[1]
    col_width = weights.shape[2]
    row_blocks = planes * points // row_width
    col_blocks = strengths.shape[0] // col_width
    slot_rows = block_rows[0, 0]
    slot_cols = block_cols[0, 0]
    live_total = block_counts[0, 0]
    live_weight = (jnp.arange(slot_total, dtype=jnp.int32) < live_total).astype(jnp.float32)
    picked = jnp.take(slab_states.reshape(state_total, row_blocks, row_width), slot_rows, axis=1)
    projected = jnp.einsum("skr,krc->kcs", picked, weights, preferred_element_type=jnp.float32)
    projected = projected * live_weight[:, None, None]
    partial_value = (
        jnp.zeros((3 * col_blocks, col_width, state_total), jnp.float32)
        .at[slot_cols]
        .add(projected)
    )
    partial_value = partial_value.reshape(3, col_blocks, col_width, state_total)
    scaling = strengths.reshape(col_blocks, col_width, 1)
    summed = lax.psum(partial_value, "band")
    below_part = passed_along(summed[2], "dom", 1)
    above_part = passed_along(summed[0], "dom", -1)
    scaled = (scaling * (summed[1] + below_part + above_part)).astype(jnp.bfloat16)
    neighbours = padded(scaled[None], (("dom", 0),), 1)
    neighbours = neighbours.reshape(3 * col_blocks, col_width, state_total)
    selected = jnp.take(neighbours, slot_cols, axis=0)
    returned = jnp.einsum("krc,kcs->skr", weights, selected, preferred_element_type=jnp.float32)
    returned = returned * live_weight[None, :, None]
    placed = (
        jnp.zeros((state_total, row_blocks, row_width), jnp.float32)
        .at[:, slot_rows, :]
        .add(returned)
    )
    result = placed.astype(jnp.bfloat16).reshape(state_total, planes, points)
    return lax.all_to_all(result, "dom", split_axis=0, concat_axis=1, tiled=True)


def solution(mesh):
    return jax.shard_map(
        per_device,
        mesh=mesh,
        in_specs=(
            P("dom", None, "band"),
            P("band", "dom", None, None, None),
            P("band", "dom", None),
            P("band", "dom", None),
            P("band", "dom"),
            P("dom"),
        ),
        out_specs=P("dom", None, "band"),
        check_vma=False,
    )
```

profile of v0, /device:TPU:25, one launch (start us, length us, event | category | flops | bytes accessed | tf_op | source)
XLA Modules:
  0.0 409.8 jit_solution(6211134194385298743)
XLA Ops:
  6.5 4.6 %copy.21 = bf16[4,512,512]{2,0,1:T(4,128)(2,1)} copy(bf16[4,512,512]{2,1,0:T(8,128)(2,1)} %param.6) | data formatting | bytes 4194304 | tf_op args[0]
  11.1 12.2 %all-to-all-start = ((bf16[4,512,512]{2,0,1:T(4,128)(2,1)}), bf16[4,512,512]{2,0,1:T(4,128)(2,1)S(1)}, u32[]{:S(2)}, u32[]{:S(2)}) async-start(bf16[4,512,512]{2,0,1:T(4,128)(2,1)} %copy.21), calls=%async_computation | async-start | bytes 4194304 | tf_op jit(solution)/shard_map/all_to_all | solution.py:27
  24.1 0.5 copy-done.2
  24.6 48.3 %all-to-all-done = bf16[4,512,512]{2,0,1:T(4,128)(2,1)S(1)} async-done(((bf16[4,512,512]{2,0,1:T(4,128)(2,1)}), bf16[4,512,512]{2,0,1:T(4,128)(2,1)S(1)}, u32[]{:S(2)}, u32[]{:S(2)}) %all-to-all-start) | async-done | bytes 2097184 | tf_op jit(solution)/shard_map/all_to_all | solution.py:27
  72.9 1.9 copy.33
  74.9 4.1 reshape.93
  78.9 2.3 copy.23
  81.2 6.8 %gather_fusion = bf16[96,256,256]{2,1,0:T(8,128)(2,1)} fusion(bf16[256,16,256]{2,0,1:T(8,128)(2,1)S(1)} %copy.23, s32[1024]{0:T(1024)S(1)} %pad_clamp_fusion.1), kind=kCustom, calls=%fused_computation | custom fusion | bytes 25166208 | tf_op jit(solution)/shard_map/jit(_take)/gather | solution.py:41
  88.0 14.4 %multiply_bitcast_fusion = f32[96,128,256]{1,2,0:T(8,128)} fusion(f32[96]{0:T(128)S(1)} %get-tuple-element.7, bf16[1,1,96,256,128]{4,3,2,1,0:T(8,128)(2,1)} %param.7, bf16[96,256,256]{2,1,0:T(8,128)(2,1)} %gather_fusion, pred[96]{0:T(512)(128)(4,1)S(1)} %get-tuple-element.8), kind=kOutput, calls=%fused_computation.8 | convolution fusion | flops 1620049920 | bytes 31457760 | tf_op jit(solution)/shard_map/skr,krc->kcs/dot_general | solution.py:42
  102.4 12.6 %copy.24 = f32[96,128,256]{2,1,0:T(8,128)} copy(f32[96,128,256]{1,2,0:T(8,128)} %multiply_bitcast_fusion) | data formatting | bytes 25165824 | tf_op jit(solution)/shard_map/mul | solution.py:43
  115.0 0.4 broadcast_in_dim.35
  115.4 18.4 %scatter_fusion = f32[27,128,256]{2,1,0:T(8,128)S(1)} fusion(f32[27,128,256]{2,1,0:T(8,128)S(1)} %broadcast_in_dim.35, s32[96]{0:T(128)S(1)} %fusion.23, f32[96,128,256]{2,1,0:T(8,128)} %copy.24), kind=kCustom, calls=%fused_computation.2 | custom fusion | flops 3145728 | bytes 37749120 | tf_op jit(solution)/shard_map/scatter-add | solution.py:47
  133.8 1.8 copy-done
  135.7 85.0 %all-reduce.2.cloned.1.call-done = f32[3,9,128,256]{3,2,1,0:T(8,128)} async-done(((f32[3,9,128,256]{3,2,1,0:T(8,128)}), f32[3,9,128,256]{3,2,1,0:T(8,128)}) %all-reduce.2.cloned.1.call-update) | async-done | bytes 3538960 | tf_op jit(solution)/shard_map/psum | solution.py:51
  220.6 1.8 slice_bitcast_fusion.1
  222.5 2.0 collective-permute-start
  224.5 13.1 %collective-permute-done = f32[9,128,256]{2,1,0:T(8,128)S(1)} collective-permute-done((f32[9,128,256]{2,1,0:T(8,128)S(1)}, f32[9,128,256]{2,1,0:T(8,128)S(1)}, u32[]{:S(2)}, u32[]{:S(2)}) %collective-permute-start) | collective-permute-done | bytes 1179680 | tf_op jit(solution)/shard_map/ppermute | solution.py:10
  237.6 4.6 %collective-permute-done.1 = f32[9,128,256]{2,1,0:T(8,128)S(1)} collective-permute-done((f32[9,128,256]{2,1,0:T(8,128)S(1)}, f32[9,128,256]{2,1,0:T(8,128)S(1)}, u32[]{:S(2)}, u32[]{:S(2)}) %collective-permute-start.1) | collective-permute-done | bytes 1179680 | tf_op jit(solution)/shard_map/ppermute | solution.py:10
  242.2 1.6 fusion.21
  243.9 0.5 collective-permute-start.3
  244.4 6.3 %collective-permute-done.2 = bf16[1,9,128,256]{3,2,1,0:T(8,128)(2,1)S(1)} collective-permute-done((bf16[1,9,128,256]{3,2,1,0:T(8,128)(2,1)S(1)}, bf16[1,9,128,256]{3,2,1,0:T(8,128)(2,1)S(1)}, u32[]{:S(2)}, u32[]{:S(2)}) %collective-permute-start.2) | collective-permute-done | bytes 589856 | tf_op jit(solution)/shard_map/ppermute | solution.py:20
  250.7 4.7 %collective-permute-done.3 = bf16[1,9,128,256]{3,2,1,0:T(8,128)(2,1)S(1)} collective-permute-done((bf16[1,9,128,256]{3,2,1,0:T(8,128)(2,1)S(1)}, bf16[1,9,128,256]{3,2,1,0:T(8,128)(2,1)S(1)}, u32[]{:S(2)}, u32[]{:S(2)}) %collective-permute-start.3) | collective-permute-done | bytes 589856 | tf_op jit(solution)/shard_map/ppermute | solution.py:21
  255.4 0.2 pad_maximum_fusion
  255.6 6.0 %gather_fusion.1 = bf16[96,128,256]{2,1,0:T(8,128)(2,1)} fusion(bf16[27,128,256]{2,1,0:T(8,128)(2,1)S(1)} %bitcast.65, s32[1024]{0:T(1024)S(1)} %pad_clamp_fusion), kind=kCustom, calls=%fused_computation.1 | custom fusion | bytes 12583296 | tf_op jit(solution)/shard_map/jit(_take)/gather | solution.py:57
  261.6 14.3 %broadcast_multiply_fusion = f32[96,256,256]{2,1,0:T(8,128)} fusion(f32[96]{0:T(128)S(1)} %get-tuple-element.7, bf16[1,1,96,256,128]{4,3,2,1,0:T(8,128)(2,1)} %param.7, bf16[96,128,256]{2,1,0:T(8,128)(2,1)} %gather_fusion.1, pred[96]{0:T(512)(128)(4,1)S(1)} %compare_and_fusion.1), kind=kOutput, calls=%fused_computation.7 | convolution fusion | flops 1620049920 | bytes 37749216 | tf_op jit(solution)/shard_map/krc,kcs->skr/dot_general | solution.py:58
  275.9 2.4 broadcast_in_dim.33
  278.3 54.0 %scatter_fusion.1 = f32[256,16,256]{2,0,1:T(8,128)} fusion(f32[256,16,256]{2,0,1:T(8,128)} %broadcast_in_dim.33, s32[96]{0:T(128)S(1)} %copy-done.3, f32[96,256,256]{2,1,0:T(8,128)} %broadcast_multiply_fusion), kind=kCustom, calls=%fused_computation.3 | custom fusion | flops 6291456 | bytes 75497856 | tf_op jit(solution)/shard_map/scatter-add | solution.py:63
  332.3 2.4 convert_element_type.19
  334.8 2.4 copy.26
  337.2 3.4 copy.27
  340.5 60.9 %all_to_all.33 = bf16[256,8,512]{2,1,0:T(8,128)(2,1)S(1)} all-to-all(bf16[256,8,512]{2,1,0:T(8,128)(2,1)S(1)} %copy.27), channel_id=1, replica_groups=mesh['band'=4,'dom'=64] {'dom'}, dimensions={0} | all-to-all | bytes 4194304 | tf_op jit(solution)/shard_map/all_to_all | solution.py:66
  401.4 1.5 copy.32
  (22 shorter events, 0.2 us)
Async XLA Ops:
  6.5 17.5 %copy-start.4 = (s32[1,1,96]{2,1,0:T(1,128)S(1)}, s32[1,1,96]{2,1,0:T(1,128)}, u32[]{:S(2)}) copy-start(s32[1,1,96]{2,1,0:T(1,128)} %param.8) | copy-start | bytes 1156
  6.5 17.5 %copy-start.5 = (s32[1,1,96]{2,1,0:T(1,128)S(1)}, s32[1,1,96]{2,1,0:T(1,128)}, u32[]{:S(2)}) copy-start(s32[1,1,96]{2,1,0:T(1,128)} %param.9) | copy-start | bytes 1156
  11.1 61.8 %all-to-all-start = ((bf16[4,512,512]{2,0,1:T(4,128)(2,1)}), bf16[4,512,512]{2,0,1:T(4,128)(2,1)S(1)}, u32[]{:S(2)}, u32[]{:S(2)}) async-start(bf16[4,512,512]{2,0,1:T(4,128)(2,1)} %copy.21), calls=%async_computation | async-start | bytes 4194304 | tf_op jit(solution)/shard_map/all_to_all | solution.py:27
  23.3 197.3 %all-reduce.2.cloned.1.call-start = ((), (), s32[]{:S(2)}) async-start(), calls=%async_computation.2 | async-start | bytes 7077888 | tf_op jit(solution)/shard_map/psum | solution.py:51
  24.0 0.6 copy-start.2
  133.8 1.8 copy-start
  133.8 108.4 %copy-start.1 = (f32[1152]{0:T(1024)S(1)}, f32[1152]{0:T(1024)}, u32[]{:S(2)}) copy-start(f32[1152]{0:T(1024)} %param.11) | copy-start | bytes 13828
  135.6 108.7 %copy-start.6 = (s32[1,1,96]{2,1,0:T(1,128)S(1)}, s32[1,1,96]{2,1,0:T(1,128)}, u32[]{:S(2)}) copy-start(s32[1,1,96]{2,1,0:T(1,128)} %param.9) | copy-start | bytes 1156
  222.5 15.2 %collective-permute-start = (f32[9,128,256]{2,1,0:T(8,128)S(1)}, f32[9,128,256]{2,1,0:T(8,128)S(1)}, u32[]{:S(2)}, u32[]{:S(2)}) collective-permute-start(f32[9,128,256]{2,1,0:T(8,128)S(1)} %get-tuple-element.5), channel_id=1, source_target_pairs={{0,1},{1,2},{2,3},{3,4},{4,5},{5,6},{6,7},{7,8},{8,9},{9,10},{10,1... | collective-permute-start | bytes 3538952 | tf_op jit(solution)/shard_map/ppermute | solution.py:10
  224.5 17.7 %collective-permute-start.1 = (f32[9,128,256]{2,1,0:T(8,128)S(1)}, f32[9,128,256]{2,1,0:T(8,128)S(1)}, u32[]{:S(2)}, u32[]{:S(2)}) collective-permute-start(f32[9,128,256]{2,1,0:T(8,128)S(1)} %get-tuple-element.6), channel_id=1, source_target_pairs={{0,63},{1,0},{2,1},{3,2},{4,3},{5,4},{6,5},{7,6},{8,7},{9,8},{10,9... | collective-permute-start | bytes 3538952 | tf_op jit(solution)/shard_map/ppermute | solution.py:10
  243.8 6.9 %collective-permute-start.2 = (bf16[1,9,128,256]{3,2,1,0:T(8,128)(2,1)S(1)}, bf16[1,9,128,256]{3,2,1,0:T(8,128)(2,1)S(1)}, u32[]{:S(2)}, u32[]{:S(2)}) collective-permute-start(bf16[1,9,128,256]{3,2,1,0:T(8,128)(2,1)S(1)} %fusion.21), channel_id=1, source_target_pairs={{0,1},{1,2},{2,3},{3,4},{4,5},{5,6},{6,7},{7,8},{8,9},{9,10},{10,1... | collective-permute-start | bytes 1769480 | tf_op jit(solution)/shard_map/ppermute | solution.py:20
  243.9 11.5 %collective-permute-start.3 = (bf16[1,9,128,256]{3,2,1,0:T(8,128)(2,1)S(1)}, bf16[1,9,128,256]{3,2,1,0:T(8,128)(2,1)S(1)}, u32[]{:S(2)}, u32[]{:S(2)}) collective-permute-start(bf16[1,9,128,256]{3,2,1,0:T(8,128)(2,1)S(1)} %fusion.21), channel_id=1, source_target_pairs={{1,0},{2,1},{3,2},{4,3},{5,4},{6,5},{7,6},{8,7},{9,8},{10,9},{11,1... | collective-permute-start | bytes 1769480 | tf_op jit(solution)/shard_map/ppermute | solution.py:21
  275.9 2.4 copy-start.3
Sparse Core Ops, SparseCore 0:
  135.8 84.8 all-reduce.1
where the time goes:
time: 412 us; the launch traced here: 410 us
  waiting for transfers between devices  162 us (39%)
  other arithmetic  76.7 us (19%)
  blocking collectives  60.9 us (15%)
  local copies, waits for them, and re-layouts  52.5 us (13%)
  matrix products  28.7 us (7%)
  starting transfers between devices  14.8 us (4%)
  between operations  14.2 us (3%)
    psum x1, waiting for transfers between devices, per_device(): summed = lax.psum(partial_value, 'band')  85 us
    all_to_all x1, blocking collectives, per_device(): lax.all_to_all(result, 'dom', split_axis=0, concat_axis=1, tiled=True)  60.9 us
    scatter-add x1, other arithmetic, per_device(): placed = jnp.zeros((state_total, row_blocks, row_width), jnp.float32).at[...  54 us
    all_to_all x1, waiting for transfers between devices, per_device(): lax.all_to_all(orbitals, 'dom', split_axis=1, concat_axis=0, tiled=True)  48.3 us
    scatter-add x1, other arithmetic, per_device(): partial_value = jnp.zeros((3 * col_blocks, col_width, state_total), jnp.f...  18.4 us
    ppermute x2, waiting for transfers between devices, passed_along(): return lax.ppermute(value, axis, pairs)  17.7 us
    dot_general x1, matrix products, per_device(): jnp.einsum('skr,krc->kcs', picked, weights, preferred_element_type=jnp.fl...  14.4 us
    dot_general x1, matrix products, per_device(): jnp.einsum('krc,kcs->skr', weights, selected, preferred_element_type=jnp....  14.3 us
  transfers between devices with their start and end apart: 6, of which 6 were waited for; matrix products, arithmetic and copies ran while one was open for 0% of the time, Pallas kernels for 0%

commit v1 on v0

v1 whole, which is shorter than its diff:
```python
import jax
import jax.numpy as jnp
from jax import lax
from jax.experimental import pallas as pl
from jax.experimental.pallas import tpu as pltpu
from jax.sharding import PartitionSpec as P


def passed_along(value, axis, steps):
    count = lax.axis_size(axis)
    pairs = [(source, (source + steps) % count) for source in range(count)]
    return lax.ppermute(value, axis, pairs)


def project_kernel(rows_ref, cols_ref, count_ref, states_ref, weights_ref, out_ref):
    out_ref[...] = jnp.zeros_like(out_ref)

    def body(k, carry):
        row = rows_ref[k]
        col = cols_ref[k]
        out_ref[col] += jnp.dot(states_ref[row], weights_ref[k], preferred_element_type=jnp.float32)
        return carry

    lax.fori_loop(0, count_ref[0], body, 0)


def apply_kernel(rows_ref, cols_ref, count_ref, chi_ref, weights_ref, out_ref, acc_ref):
    acc_ref[...] = jnp.zeros_like(acc_ref)

    def body(k, carry):
        row = rows_ref[k]
        col = cols_ref[k]
        acc_ref[row] += lax.dot_general(
            chi_ref[col], weights_ref[k], (((1,), (1,)), ((), ())), preferred_element_type=jnp.float32
        )
        return carry

    lax.fori_loop(0, count_ref[0], body, 0)
    out_ref[...] = acc_ref[...].astype(out_ref.dtype)


def smem():
    return pl.BlockSpec(memory_space=pltpu.SMEM)


def vmem():
    return pl.BlockSpec(memory_space=pltpu.VMEM)


def project(rows, cols, count, states, weights, col_blocks):
    row_blocks, state_total, row_width = states.shape
    slot_total, _, col_width = weights.shape
    flops = 2 * slot_total * state_total * row_width * col_width
    moved = states.size * 2 + weights.size * 2 + col_blocks * state_total * col_width * 4
    return pl.pallas_call(
        project_kernel,
        out_shape=jax.ShapeDtypeStruct((col_blocks, state_total, col_width), jnp.float32),
        in_specs=[smem(), smem(), smem(), vmem(), vmem()],
        out_specs=vmem(),
        compiler_params=pltpu.CompilerParams(vmem_limit_bytes=60 * 1024 * 1024),
        cost_estimate=pl.CostEstimate(flops=flops, bytes_accessed=moved, transcendentals=0),
    )(rows, cols, count, states, weights)


def apply(rows, cols, count, chi, weights, row_blocks):
    col_blocks, state_total, col_width = chi.shape
    slot_total, row_width, _ = weights.shape
    flops = 2 * slot_total * state_total * row_width * col_width
    moved = chi.size * 2 + weights.size * 2 + row_blocks * state_total * row_width * 2
    return pl.pallas_call(
        apply_kernel,
        out_shape=jax.ShapeDtypeStruct((row_blocks, state_total, row_width), jnp.bfloat16),
        in_specs=[smem(), smem(), smem(), vmem(), vmem()],
        out_specs=vmem(),
        scratch_shapes=[pltpu.VMEM((row_blocks, state_total, row_width), jnp.float32)],
        compiler_params=pltpu.CompilerParams(vmem_limit_bytes=60 * 1024 * 1024),
        cost_estimate=pl.CostEstimate(flops=flops, bytes_accessed=moved, transcendentals=0),
    )(rows, cols, count, chi, weights)


def per_device(orbitals, projector_blocks, block_rows, block_cols, block_counts, strengths):
    dom = lax.axis_size("dom")
    local_states, planes_all, points = orbitals.shape
    planes = planes_all // dom
    weights = projector_blocks[0, 0]
    slot_total, row_width, col_width = weights.shape
    halves = points // row_width
    row_blocks = planes * halves
    col_blocks = strengths.shape[0] // col_width
    state_total = local_states * dom

    outgoing = orbitals.reshape(local_states, dom, planes, halves, row_width).transpose(1, 2, 3, 0, 4)
    slab_states = lax.all_to_all(outgoing, "dom", split_axis=0, concat_axis=3, tiled=True)
    slab_states = slab_states.reshape(row_blocks, state_total, row_width)

    slot_rows = block_rows[0, 0]
    slot_cols = block_cols[0, 0]
    live_total = block_counts[0, 0].reshape(1)

    partial_value = project(slot_rows, slot_cols, live_total, slab_states, weights, 3 * col_blocks)
    partial_value = partial_value.reshape(3, col_blocks, state_total, col_width)
    from_below = passed_along(partial_value[2], "dom", 1)
    from_above = passed_along(partial_value[0], "dom", -1)
    own = partial_value[1] + from_below + from_above
    summed = lax.psum(own, "band")
    scaling = strengths.reshape(col_blocks, 1, col_width)
    scaled = (scaling * summed).astype(jnp.bfloat16)
    chi_below = passed_along(scaled, "dom", 1)
    chi_above = passed_along(scaled, "dom", -1)
    neighbours = jnp.concatenate([chi_below, scaled, chi_above], axis=0)

    applied = apply(slot_rows, slot_cols, live_total, neighbours, weights, row_blocks)
    applied = applied.reshape(1, planes, halves, state_total, row_width)
    returned = lax.all_to_all(applied, "dom", split_axis=3, concat_axis=0, tiled=True)
    returned = returned.transpose(3, 0, 1, 2, 4)
    return returned.reshape(local_states, planes_all, points)


def solution(mesh):
    return jax.shard_map(
        per_device,
        mesh=mesh,
        in_specs=(
            P("dom", None, "band"),
            P("band", "dom", None, None, None),
            P("band", "dom", None),
            P("band", "dom", None),
            P("band", "dom"),
            P("dom"),
        ),
        out_specs=P("dom", None, "band"),
        check_vma=False,
    )
```

time: 412 us -> 286 us (0.69)
  other arithmetic: 76.7 us -> 5.31 us
  local copies, waits for them, and re-layouts: 52.5 us -> 20.2 us
  matrix products: 28.7 us -> 0 us
  waiting for transfers between devices: 162 us -> 135 us
  Pallas kernels: 0 us -> 16.6 us
  blocking collectives: 60.9 us -> 74 us
    scatter-add x2 -> x0, other arithmetic: 72.4 us -> none  [the longest x1 54 us: per_device(): placed = jnp.zeros((state_total, row_blocks, row_width), jnp.float32).at[...]
    dot_general x2 -> x0, matrix products: 28.7 us -> none  [the longest x1 14.4 us: per_device(): jnp.einsum('skr,krc->kcs', picked, weights, preferred_element_type=jnp.fl...]
    psum x1, waiting for transfers between devices: 85 us -> 61 us  [per_device(): summed = lax.psum(own, 'band')]
    pallas_call x0 -> x2, Pallas kernels: none -> 16.6 us  [the longest x1 8.34 us: apply(): pl.pallas_call(apply_kernel, out_shape=jax.ShapeDtypeStruct((row_blocks,...]
    all_to_all x1, blocking collectives: 60.9 us -> 74 us  [per_device(): lax.all_to_all(applied, 'dom', split_axis=3, concat_axis=0, tiled=True)]
    gather x2 -> x0, local copies, waits for them, and re-layouts: 12.8 us -> none  [the longest x1 6.78 us: per_device(): jnp.take(slab_states.reshape(state_total, row_blocks, row_width), slot_ro...]
    mul x1 -> x0, local copies, waits for them, and re-layouts: 12.6 us -> none  [per_device(): projected = projected * live_weight[:, None, None]]
    ppermute x2 -> x0, waiting for transfers between devices: 11 us -> none  [the longest x1 6.3 us: padded(): before = lax.ppermute(last, axis, up)]
  transfers between devices with their start and end apart: 6 -> 6, of which waited for: 6 -> 5; matrix products, arithmetic and copies ran while one was open for 0% -> 0% of each run, Pallas kernels for 0% -> 0%
where the time goes in v1:
time: 286 us; the launch traced here: 284 us
  waiting for transfers between devices  135 us (47%)
  blocking collectives  74 us (26%)
  local copies, waits for them, and re-layouts  20.2 us (7%)
  starting transfers between devices  18.6 us (7%)
  Pallas kernels  16.6 us (6%)
  between operations  14.1 us (5%)
  other arithmetic  5.31 us (2%)
    all_to_all x1, blocking collectives, per_device(): lax.all_to_all(applied, 'dom', split_axis=3, concat_axis=0, tiled=True)  74 us
    psum x1, waiting for transfers between devices, per_device(): summed = lax.psum(own, 'band')  61 us
    all_to_all x1, waiting for transfers between devices, per_device(): lax.all_to_all(outgoing, 'dom', split_axis=0, concat_axis=3, tiled=True)  48.9 us
    ppermute x4, waiting for transfers between devices, passed_along(): return lax.ppermute(value, axis, pairs)  25.3 us
    all_to_all x1, starting transfers between devices, per_device(): lax.all_to_all(outgoing, 'dom', split_axis=0, concat_axis=3, tiled=True)  12.2 us
    pallas_call x1, Pallas kernels, apply(): pl.pallas_call(apply_kernel, out_shape=jax.ShapeDtypeStruct((row_blocks,...  8.34 us
    pallas_call x1, Pallas kernels, project(): pl.pallas_call(project_kernel, out_shape=jax.ShapeDtypeStruct((col_blocks...  8.21 us
    ppermute x4, starting transfers between devices, passed_along(): return lax.ppermute(value, axis, pairs)  6.37 us
  transfers between devices with their start and end apart: 6, of which 5 were waited for; matrix products, arithmetic and copies ran while one was open for 0% of the time, Pallas kernels for 0%

profile of v1, /device:TPU:25, one launch (start us, length us, event | category | flops | bytes accessed | tf_op | source)
XLA Modules:
  0.0 284.0 jit_solution(4381613521850630023)
XLA Ops:
  6.5 2.5 reshape.22
  9.1 4.0 %copy.12 = bf16[64,8,2,4,256]{4,3,2,1,0:T(4,128)(2,1)} copy(bf16[64,8,2,4,256]{4,2,1,0,3:T(2,128)(2,1)S(1)} %bitcast.24) | data formatting | bytes 4194304 | tf_op jit(solution)/shard_map/transpose | solution.py:92
  13.1 12.2 %all-to-all-start = ((bf16[64,8,2,4,256]{4,3,2,1,0:T(4,128)(2,1)}), bf16[64,8,2,4,256]{4,3,2,1,0:T(4,128)(2,1)S(1)}, u32[]{:S(2)}, u32[]{:S(2)}) async-start(bf16[64,8,2,4,256]{4,3,2,1,0:T(4,128)(2,1)} %copy.12), calls=%async_computation | async-start | bytes 4194304 | tf_op jit(solution)/shard_map/all_to_all | solution.py:93
  25.3 0.0 all-reduce.2.cloned.1.call-start
  26.0 48.9 %all-to-all-done = bf16[64,8,2,4,256]{4,3,2,1,0:T(4,128)(2,1)S(1)} async-done(((bf16[64,8,2,4,256]{4,3,2,1,0:T(4,128)(2,1)}), bf16[64,8,2,4,256]{4,3,2,1,0:T(4,128)(2,1)S(1)}, u32[]{:S(2)}, u32[]{:S(2)}) %all-to-all-start) | async-done | bytes 2097184 | tf_op jit(solution)/shard_map/all_to_all | solution.py:93
  74.9 2.3 copy.13
  77.3 4.0 %reshape.23.states_ref = bf16[16,256,256]{2,1,0:T(8,128)(2,1)} reshape(bf16[1,8,2,64,4,256]{5,4,3,2,1,0:T(4,128)(2,1)} %copy.13) | data formatting | bytes 4194304 | tf_op jit(solution)/shard_map/reshape | solution.py:94
  81.3 8.2 %shard_map.64 = f32[27,256,128]{2,1,0:T(8,128)} custom-call(s32[96]{0:T(128)} %bitcast.27, s32[96]{0:T(128)} %bitcast.29, s32[1]{0:T(128)} %bitcast.18.count_ref, bf16[16,256,256]{2,1,0:T(8,128)(2,1)} %reshape.23.states_ref, bf16[96,256,128]{2,1,0:T(8,128)(2,1)} %bitcast.20), custom_call_target="tpu_custom_call" | custom-call | flops 1610612736 | bytes 11927552 | tf_op jit(solution)/shard_map/pallas_call | solution.py:55
  89.5 1.8 fusion.1
  91.3 2.4 collective-permute-start
  93.7 0.0 copy-start
  93.7 0.0 collective-permute-start.1
  93.7 13.1 %collective-permute-done = f32[9,256,128]{2,1,0:T(8,128)S(1)} collective-permute-done((f32[9,256,128]{2,1,0:T(8,128)S(1)}, f32[9,256,128]{2,1,0:T(8,128)S(1)}, u32[]{:S(2)}, u32[]{:S(2)}) %collective-permute-start) | collective-permute-done | bytes 1179680 | tf_op jit(solution)/shard_map/ppermute | solution.py:12
  106.8 4.6 %collective-permute-done.1 = f32[9,256,128]{2,1,0:T(8,128)S(1)} collective-permute-done((f32[9,256,128]{2,1,0:T(8,128)S(1)}, f32[9,256,128]{2,1,0:T(8,128)S(1)}, u32[]{:S(2)}, u32[]{:S(2)}) %collective-permute-start.1) | collective-permute-done | bytes 1179680 | tf_op jit(solution)/shard_map/ppermute | solution.py:12
  111.4 2.5 fusion
  113.9 0.0 all-reduce.2.cloned.1.call-update
  114.0 61.0 %all-reduce.2.cloned.1.call-done = f32[9,256,128]{2,1,0:T(8,128)} async-done(((f32[9,256,128]{2,1,0:T(8,128)}), f32[9,256,128]{2,1,0:T(8,128)}) %all-reduce.2.cloned.1.call-update) | async-done | bytes 1179664 | tf_op jit(solution)/shard_map/psum | solution.py:105
  174.9 0.0 copy-done
  174.9 1.4 multiply_convert_fusion
  176.3 1.9 collective-permute-start.3
  178.2 2.1 collective-permute-start.2
  180.2 7.6 %collective-permute-done.3 = bf16[9,256,128]{2,1,0:T(8,128)(2,1)S(1)} collective-permute-done((bf16[9,256,128]{2,1,0:T(8,128)(2,1)S(1)}, bf16[9,256,128]{2,1,0:T(8,128)(2,1)S(1)}, u32[]{:S(2)}, u32[]{:S(2)}) %collective-permute-start.3) | collective-permute-done | bytes 589856 | tf_op jit(solution)/shard_map/ppermute | solution.py:12
  187.8 0.0 collective-permute-done.2
  187.8 1.4 pad_maximum_fusion.chi_ref
  189.2 8.3 %shard_map.65 = bf16[16,256,256]{2,1,0:T(8,128)(2,1)} custom-call(s32[96]{0:T(128)} %bitcast.28, s32[96]{0:T(128)} %bitcast.30, s32[1]{0:T(128)} %bitcast.19.count_ref, bf16[27,256,128]{2,1,0:T(8,128)(2,1)} %pad_maximum_fusion.chi_ref, bf16[96,256,128]{2,1,0:T(8,128)(2,1)} %bitcast.21), custom_call_target="tpu_custom_call" | custom-call | flops 1610612736 | bytes 10158080 | tf_op jit(solution)/shard_map/pallas_call | solution.py:70
  197.6 3.7 %copy.14 = bf16[1,8,2,256,256]{4,2,1,0,3:T(2,128)(2,1)S(1)} copy(bf16[1,8,2,256,256]{4,3,2,1,0:T(8,128)(2,1)} %bitcast.25) | data formatting | bytes 4194304 | tf_op jit(solution)/shard_map/reshape | solution.py:113
  201.3 74.0 %all_to_all.33 = bf16[1,8,2,256,256]{4,2,1,0,3:T(2,128)(2,1)S(1)} all-to-all(bf16[1,8,2,256,256]{4,2,1,0,3:T(2,128)(2,1)S(1)} %copy.14), channel_id=1, replica_groups=mesh['band'=4,'dom'=64] {'dom'}, dimensions={3} | all-to-all | bytes 4194304 | tf_op jit(solution)/shard_map/all_to_all | solution.py:114
  275.3 1.8 copy.15
Async XLA Ops:
  13.1 61.8 %all-to-all-start = ((bf16[64,8,2,4,256]{4,3,2,1,0:T(4,128)(2,1)}), bf16[64,8,2,4,256]{4,3,2,1,0:T(4,128)(2,1)S(1)}, u32[]{:S(2)}, u32[]{:S(2)}) async-start(bf16[64,8,2,4,256]{4,3,2,1,0:T(4,128)(2,1)} %copy.12), calls=%async_computation | async-start | bytes 4194304 | tf_op jit(solution)/shard_map/all_to_all | solution.py:93
  25.3 149.6 %all-reduce.2.cloned.1.call-start = ((), (), s32[]{:S(2)}) async-start(), calls=%async_computation.2 | async-start | bytes 2359296 | tf_op jit(solution)/shard_map/psum | solution.py:105
  91.3 15.6 %collective-permute-start = (f32[9,256,128]{2,1,0:T(8,128)S(1)}, f32[9,256,128]{2,1,0:T(8,128)S(1)}, u32[]{:S(2)}, u32[]{:S(2)}) collective-permute-start(f32[9,256,128]{2,1,0:T(8,128)S(1)} %get-tuple-element.5), channel_id=1, source_target_pairs={{0,1},{1,2},{2,3},{3,4},{4,5},{5,6},{6,7},{7,8},{8,9},{9,10},{10,1... | collective-permute-start | bytes 3538952 | tf_op jit(solution)/shard_map/ppermute | solution.py:12
  93.7 81.2 %copy-start = (f32[1152]{0:T(1024)S(1)}, f32[1152]{0:T(1024)}, u32[]{:S(2)}) copy-start(f32[1152]{0:T(1024)} %param.11) | copy-start | bytes 13828
  93.7 17.7 %collective-permute-start.1 = (f32[9,256,128]{2,1,0:T(8,128)S(1)}, f32[9,256,128]{2,1,0:T(8,128)S(1)}, u32[]{:S(2)}, u32[]{:S(2)}) collective-permute-start(f32[9,256,128]{2,1,0:T(8,128)S(1)} %get-tuple-element.6), channel_id=1, source_target_pairs={{0,63},{1,0},{2,1},{3,2},{4,3},{5,4},{6,5},{7,6},{8,7},{9,8},{10,9... | collective-permute-start | bytes 3538952 | tf_op jit(solution)/shard_map/ppermute | solution.py:12
  176.3 11.5 %collective-permute-start.3 = (bf16[9,256,128]{2,1,0:T(8,128)(2,1)S(1)}, bf16[9,256,128]{2,1,0:T(8,128)(2,1)S(1)}, u32[]{:S(2)}, u32[]{:S(2)}) collective-permute-start(bf16[9,256,128]{2,1,0:T(8,128)(2,1)S(1)} %multiply_convert_fusion), channel_id=1, source_target_pairs={{0,63},{1,0},{2,1},{3,2},{4,3},{5,4},{6,5},{7,6},{8,7},{9,8},{10,9... | collective-permute-start | bytes 1769480 | tf_op jit(solution)/shard_map/ppermute | solution.py:12
  178.2 9.6 %collective-permute-start.2 = (bf16[9,256,128]{2,1,0:T(8,128)(2,1)S(1)}, bf16[9,256,128]{2,1,0:T(8,128)(2,1)S(1)}, u32[]{:S(2)}, u32[]{:S(2)}) collective-permute-start(bf16[9,256,128]{2,1,0:T(8,128)(2,1)S(1)} %multiply_convert_fusion), channel_id=1, source_target_pairs={{0,1},{1,2},{2,3},{3,4},{4,5},{5,6},{6,7},{7,8},{8,9},{9,10},{10,1... | collective-permute-start | bytes 1769480 | tf_op jit(solution)/shard_map/ppermute | solution.py:12
Sparse Core Ops, SparseCore 0:
  114.1 60.7 all-reduce.1
